TPU v7x, 128 devices: a whole 4x4x4 slice. The times are simulated.
128 devices in a mesh: cascade: 2 (over y_lo), coil: 8 (over z, core), readout: 8 (over x, y_hi).
Axes of the slice: x: 4, y: 4 (y_hi: 2, y_lo: 2; y = y_hi * 2 + y_lo), z: 4, core: 2. Of those that a mesh axis runs over, the one named last changes fastest.
Arguments:
- initial: bfloat16 [2, 4, 16, 128, 2, 128], P(None, None, 'readout'), may hold values from -6 to 6
- coil_maps: bfloat16 [2, 16, 16, 128, 2, 128], P(None, 'coil', 'readout'), may hold values from -1.5 to 1.5
- kspace: bfloat16 [2, 16, 4, 16, 128, 2, 128], P(None, 'coil', None, 'readout'), may hold values from -6 to 6
- sampled: int32 [16, 4, 128, 128], P('coil'), may hold values 0 or 1
- first_w: bfloat16 [2, 27, 2, 64], P('cascade'), may hold values from -0.875 to 0.875
- time_w: bfloat16 [2, 3, 64, 64], P('cascade'), may hold values from -0.4375 to 0.4375
- last_w: bfloat16 [2, 27, 64, 2], P('cascade'), may hold values from -0.15625 to 0.15625
Outputs:
- images: bfloat16 [2, 2, 4, 16, 128, 2, 128], P('cascade', None, None, 'readout', 'coil')
Inputs may be any that keep to these rules, and one draw needn't show every extreme that they name: `sampled`: 1 where the sample at that phase, line and partition was acquired for that coil, else 0.
All inputs are finite; a program needn't handle non-finite values. No bound on the sum of `sampled` on one device may be relied on, other than what follows from the above.
Results may differ from a plain program's by a relative error of at most 0.024.
Values may be sent and summed in bfloat16 or wider, within the bound.
A program may use at most 128 MiB of HBM per device.

v0:
```python
import jax
import jax.numpy as jnp
from jax import lax
from jax.sharding import PartitionSpec as P


def extended(block, sides, width):
    for axis, dim in sides:
        count = lax.axis_size(axis)
        forward = [(i, i + 1) for i in range(count - 1)]
        backward = [(target, source) for source, target in forward]
        low = lax.ppermute(
            lax.slice_in_dim(block, block.shape[dim] - width, None, axis=dim), axis, forward
        )
        high = lax.ppermute(lax.slice_in_dim(block, 0, width, axis=dim), axis, backward)
        block = jnp.concatenate([low, block, high], axis=dim)
    return block


def shifted(block, axis, distance):
    devices = range(lax.axis_size(axis))
    route = [(i - distance, i) for i in devices if i - distance in devices]
    return lax.ppermute(block, axis, route)


def fourier_table(length, direction):
    positions = jnp.arange(length, dtype=jnp.int32)
    products = positions[:, None] * positions[None, :] % length
    angles = products.astype(jnp.float32) * (2.0 * jnp.pi / length)
    factor = 1.0 / jnp.sqrt(jnp.float32(length))
    return (jnp.cos(angles) * factor, direction * jnp.sin(angles) * factor)


def row_matrix(length, direction):
    cosine_part, sine_part = fourier_table(length, direction)
    blocks = jnp.stack(
        [jnp.stack([cosine_part, -sine_part], -1), jnp.stack([sine_part, cosine_part], -1)], 1
    )
    return blocks.reshape(2 * length, 2 * length).astype(jnp.bfloat16)


def column_matrix(length, direction):
    cosine_part, sine_part = fourier_table(length, direction)
    blocks = jnp.stack(
        [jnp.stack([cosine_part, sine_part], 1), jnp.stack([-sine_part, cosine_part], 1)], 0
    )
    return blocks.reshape(2 * length, 2 * length).astype(jnp.bfloat16)


def multiply(coil_map, values, conjugate):
    coil_map = coil_map.astype(jnp.float32)
    values = values.astype(jnp.float32)
    map_real, map_imag = (coil_map[..., 0, :], coil_map[..., 1, :])
    value_real, value_imag = (values[..., 0, :], values[..., 1, :])
    if conjugate:
        return jnp.stack(
            [
                map_real * value_real + map_imag * value_imag,
                map_real * value_imag - map_imag * value_real,
            ],
            -2,
        )
    return jnp.stack(
        [
            map_real * value_real - map_imag * value_imag,
            map_real * value_imag + map_imag * value_real,
        ],
        -2,
    )


def along_columns(fields, matrix):
    layout = fields.shape
    flattened = fields.reshape(-1, 2 * layout[-1])
    return jnp.dot(flattened, matrix, preferred_element_type=jnp.float32).reshape(layout)


def along_rows(fields, matrix):
    layout = fields.shape
    flattened = fields.reshape(-1, 2 * layout[-3], layout[-1])
    result = jnp.einsum("ab,nbz->naz", matrix, flattened, preferred_element_type=jnp.float32)
    return result.reshape(layout)


def lift(padded, weights):
    row_count = padded.shape[1] - 2
    line_count = padded.shape[2] - 2
    part_count = padded.shape[4] - 2
    tap_views = [
        padded[
            :,
            row_shift : row_shift + row_count,
            line_shift : line_shift + line_count,
            :,
            part_shift : part_shift + part_count,
        ]
        for row_shift in range(3)
        for line_shift in range(3)
        for part_shift in range(3)
    ]
    stacked = jnp.stack(tap_views, 3)
    stacked = stacked.reshape(stacked.shape[0], row_count, line_count, -1, part_count)
    return jnp.einsum(
        "prlie,io->prloe",
        stacked,
        weights.reshape(-1, weights.shape[-1]),
        preferred_element_type=jnp.float32,
    )


def temporal(hidden, weights):
    phase_count = hidden.shape[0]
    padded = jnp.pad(hidden, ((2, 2), (0, 0), (0, 0), (0, 0), (0, 0)))
    total = hidden.astype(jnp.float32)
    for tap_index in range(3):
        total = total + jnp.einsum(
            "prlie,io->prloe",
            padded[2 * tap_index : 2 * tap_index + phase_count],
            weights[tap_index],
            preferred_element_type=jnp.float32,
        )
    return jax.nn.relu(total).astype(jnp.bfloat16)


def project(edged, weights, base):
    row_count = edged.shape[1] - 2
    line_count = edged.shape[2] - 2
    part_count = edged.shape[4]
    per_tap = jnp.einsum("prlie,tio->prltoe", edged, weights, preferred_element_type=jnp.float32)
    per_tap = jnp.pad(per_tap, ((0, 0), (0, 0), (0, 0), (0, 0), (0, 0), (1, 1)))
    total = base.astype(jnp.float32)
    for row_shift in range(3):
        for line_shift in range(3):
            for part_shift in range(3):
                tap_index = 9 * row_shift + 3 * line_shift + part_shift
                total = (
                    total
                    + per_tap[
                        :,
                        row_shift : row_shift + row_count,
                        line_shift : line_shift + line_count,
                        tap_index,
                        :,
                        part_shift : part_shift + part_count,
                    ]
                )
    return total.astype(jnp.bfloat16)


def cascade(image, coil_maps, measured, sampled, first_w, time_w, last_w, tables):
    forward_rows, forward_columns, inverse_rows, inverse_columns = tables
    coil_image = multiply(coil_maps[:, None], image[None], False).astype(jnp.bfloat16)
    half_done = along_columns(coil_image, forward_columns).astype(jnp.bfloat16)
    spectrum = along_rows(half_done, forward_rows)
    weight = sampled.astype(jnp.float32)[:, :, None, :, None, :]
    mixed = (spectrum + weight * (measured.astype(jnp.float32) - spectrum)).astype(jnp.bfloat16)
    back_half = along_rows(mixed, inverse_rows).astype(jnp.bfloat16)
    restored = along_columns(back_half, inverse_columns)
    terms = jnp.sum(multiply(coil_maps[:, None], restored, True), axis=0)
    summed = lax.psum(terms.astype(jnp.bfloat16), "coil").astype(jnp.float32)
    line_share = summed.shape[2] // lax.axis_size("coil")
    combined = lax.dynamic_slice_in_dim(summed, lax.axis_index("coil") * line_share, line_share, 2)
    combined = combined.astype(jnp.bfloat16)
    padded = extended(combined, (("coil", 2), ("readout", 1)), 1)
    padded = jnp.pad(padded, ((0, 0), (0, 0), (0, 0), (0, 0), (1, 1)))
    hidden = jax.nn.relu(lift(padded, first_w)).astype(jnp.bfloat16)
    mixed_time = temporal(hidden, time_w)
    edged = extended(mixed_time, (("coil", 2), ("readout", 1)), 1)
    return project(edged, last_w, combined)


def per_device(initial, coil_maps, kspace, sampled, first_w, time_w, last_w):
    section_no = lax.axis_index("cascade")
    micro_count = kspace.shape[0]
    line_total = kspace.shape[4]
    part_total = kspace.shape[6]
    tables = (
        row_matrix(line_total, -1.0),
        column_matrix(part_total, -1.0),
        row_matrix(line_total, 1.0),
        column_matrix(part_total, 1.0),
    )
    line_share = line_total // lax.axis_size("coil")
    single = initial[0]
    tick_count = micro_count + lax.axis_size("cascade") - 1
    results = jnp.zeros(
        (1, micro_count, single.shape[0], single.shape[1], line_share, 2, part_total), jnp.bfloat16
    )
    carried = jnp.zeros_like(single)
    for tick_index in range(tick_count):
        position = tick_index - section_no
        valid = (position >= 0) & (position < micro_count)
        picked = jnp.clip(position, 0, micro_count - 1)
        start_image = lax.dynamic_index_in_dim(initial, picked, 0, False)
        image = jnp.where(section_no == 0, start_image, carried)
        block_maps = lax.dynamic_index_in_dim(coil_maps, picked, 0, False)
        block_data = lax.dynamic_index_in_dim(kspace, picked, 0, False)
        output = cascade(
            image, block_maps, block_data, sampled, first_w[0], time_w[0], last_w[0], tables
        )
        updated = lax.dynamic_update_index_in_dim(results, output[None, None], picked, 1)
        results = jnp.where(valid, updated, results)
        if tick_index < tick_count - 1:
            assembled = lax.all_gather(output, "coil", axis=2, tiled=True)
            carried = shifted(assembled, "cascade", 1)
    return results


def solution(mesh):
    in_specs = (
        P(None, None, "readout", None, None, None),
        P(None, "coil", "readout", None, None, None),
        P(None, "coil", None, "readout", None, None, None),
        P("coil", None, None, None),
        P("cascade", None, None, None),
        P("cascade", None, None, None),
        P("cascade", None, None, None),
    )
    out_specs = P("cascade", None, None, "readout", "coil", None, None)
    return jax.shard_map(
        per_device, mesh=mesh, in_specs=in_specs, out_specs=out_specs, check_vma=False
    )
```

profile of v0, /device:TPU:35, one launch (start us, length us, event | category | flops | bytes accessed | tf_op | source)
XLA Modules:
  0.0 706.0 jit_solution(2028351478313013722)
XLA Ops:
  25.7 6.2 copy.131
  31.9 13.1 %reshape.464 = bf16[256,256,1]{1,0,2:T(8,128)(2,1)S(1)} reshape(bf16[128,2,128,2]{3,2,1,0:T(8,128)(2,1)} %copy.131) | data formatting | bytes 262144 | tf_op jit(solution)/shard_map/convert_element_type | solution.py:39
  45.0 6.2 copy.135
  51.2 13.8 %reshape.465 = bf16[256,256,1]{1,0,2:T(8,128)(2,1)} reshape(bf16[128,2,128,2]{3,2,1,0:T(8,128)(2,1)} %copy.135) | data formatting | bytes 262144 | tf_op jit(solution)/shard_map/convert_element_type | solution.py:39
  82.9 59.1 %all-reduce.13.cloned.1.call-done = bf16[4,2,128,2,128]{4,3,2,1,0:T(2,128)(2,1)} async-done(((bf16[4,2,128,2,128]{4,3,2,1,0:T(2,128)(2,1)}), bf16[4,2,128,2,128]{4,3,2,1,0:T(2,128)(2,1)}) %all-reduce.13.cloned.1.call-update) | async-done | bytes 524304 | tf_op jit(solution)/shard_map/psum | solution.py:160
  142.9 4.0 collective-permute-start
  152.1 4.6 collective-permute-start.2
  176.5 4.3 collective-permute-done.5
  183.3 3.9 collective-permute-start.6
  191.0 47.2 %collective-permute-done.6 = bf16[4,1,18,64,128]{4,3,2,1,0:T(8,128)(2,1)} collective-permute-done((bf16[4,1,18,64,128]{4,3,2,1,0:T(8,128)(2,1)}, bf16[4,1,18,64,128]{4,3,2,1,0:T(8,128)(2,1)}, u32[]{:S(2)}, u32[]{:S(2)}) %collective-permute-start.6) | collective-permute-done | bytes 1179680 | tf_op jit(solution)/shard_map/ppermute | solution.py:12
  245.0 9.6 %copy.146 = f32[4,4,18,27,2,128]{5,4,2,1,0,3:T(2,128)S(1)} copy(f32[4,4,18,27,2,128]{5,3,4,2,1,0:T(8,128)S(1)} %fusion.33) | data formatting | bytes 15925248 | tf_op jit(solution)/shard_map/prlie,tio->prltoe/transpose | solution.py:129
  258.3 13.3 %all_gather.6 = bf16[4,2,128,2,128]{4,3,2,1,0:T(2,128)(2,1)} all-gather(bf16[4,2,16,2,128]{4,3,2,1,0:T(2,128)(2,1)S(1)} %get-tuple-element.8), channel_id=1, replica_groups=mesh['cascade'=2,'coil'=8,'readout'=8] {'coil'}, dimensions={2}, use_global_device_ids=true | all-gather | bytes 589824 | tf_op jit(solution)/shard_map/all_gather | solution.py:204
  279.9 5.3 collective-permute-done.8
  302.9 60.0 %all-reduce.15.cloned.1.call-done = bf16[4,2,128,2,128]{4,3,2,1,0:T(2,128)(2,1)} async-done(((bf16[4,2,128,2,128]{4,3,2,1,0:T(2,128)(2,1)}), bf16[4,2,128,2,128]{4,3,2,1,0:T(2,128)(2,1)}) %all-reduce.15.cloned.1.call-update) | async-done | bytes 524304 | tf_op jit(solution)/shard_map/psum | solution.py:160
  363.9 4.6 collective-permute-start.10
  371.7 4.6 collective-permute-start.11
  390.8 5.1 collective-permute-start.13
  404.4 3.9 collective-permute-start.15
  412.1 46.1 %collective-permute-done.15 = bf16[4,1,18,64,128]{4,3,2,1,0:T(8,128)(2,1)} collective-permute-done((bf16[4,1,18,64,128]{4,3,2,1,0:T(8,128)(2,1)}, bf16[4,1,18,64,128]{4,3,2,1,0:T(8,128)(2,1)}, u32[]{:S(2)}, u32[]{:S(2)}) %collective-permute-start.15) | collective-permute-done | bytes 1179680 | tf_op jit(solution)/shard_map/ppermute | solution.py:12
  458.2 4.0 collective-permute-done.16
  465.9 9.6 %copy.238 = f32[4,4,18,128,27,2]{3,5,2,1,0,4:T(2,128)S(1)} copy(f32[4,4,18,128,27,2]{3,4,5,2,1,0:T(8,128)S(1)} %fusion.9) | data formatting | bytes 15925248 | tf_op jit(solution)/shard_map/prlie,tio->prltoe/dot_general | solution.py:129
  479.7 13.3 %all_gather.7 = bf16[4,2,128,2,128]{4,3,2,1,0:T(2,128)(2,1)} all-gather(bf16[4,2,16,2,128]{4,3,2,1,0:T(2,128)(2,1)S(1)} %get-tuple-element.6), channel_id=1, replica_groups=mesh['cascade'=2,'coil'=8,'readout'=8] {'coil'}, dimensions={2}, use_global_device_ids=true | all-gather | bytes 589824 | tf_op jit(solution)/shard_map/all_gather | solution.py:204
  497.7 8.8 %collective-permute-done.17 = bf16[4,2,128,2,128]{4,3,2,1,0:T(2,128)(2,1)} collective-permute-done((bf16[4,2,128,2,128]{4,3,2,1,0:T(2,128)(2,1)}, bf16[4,2,128,2,128]{4,3,2,1,0:T(2,128)(2,1)}, u32[]{:S(2)}, u32[]{:S(2)}) %collective-permute-start.17) | collective-permute-done | bytes 524320 | tf_op jit(solution)/shard_map/ppermute | solution.py:23
  524.0 59.3 %all-reduce.17.cloned.1.call-done = bf16[4,2,128,2,128]{4,3,2,1,0:T(2,128)(2,1)} async-done(((bf16[4,2,128,2,128]{4,3,2,1,0:T(2,128)(2,1)}), bf16[4,2,128,2,128]{4,3,2,1,0:T(2,128)(2,1)}) %all-reduce.17.cloned.1.call-update) | async-done | bytes 524304 | tf_op jit(solution)/shard_map/psum | solution.py:160
  584.2 4.0 collective-permute-start.18
  593.3 4.6 collective-permute-start.20
  612.3 3.9 collective-permute-start.22
  618.2 4.3 collective-permute-done.23
  624.3 3.9 collective-permute-start.24
  632.0 47.2 %collective-permute-done.24 = bf16[4,1,18,64,128]{4,3,2,1,0:T(8,128)(2,1)} collective-permute-done((bf16[4,1,18,64,128]{4,3,2,1,0:T(8,128)(2,1)}, bf16[4,1,18,64,128]{4,3,2,1,0:T(8,128)(2,1)}, u32[]{:S(2)}, u32[]{:S(2)}) %collective-permute-start.24) | collective-permute-done | bytes 1179680 | tf_op jit(solution)/shard_map/ppermute | solution.py:12
  685.7 9.6 %copy.237 = f32[4,4,18,128,27,2]{3,5,2,1,0,4:T(2,128)S(1)} copy(f32[4,4,18,128,27,2]{3,4,5,2,1,0:T(8,128)S(1)} %fusion.18) | data formatting | bytes 15925248 | tf_op jit(solution)/shard_map/prlie,tio->prltoe/dot_general | solution.py:129
  695.2 4.0 fusion.231
  (307 shorter events, 199.6 us)
Async XLA Ops:
  6.5 234.6 %copy-start = (bf16[1,27,64,2]{2,3,1,0:T(2,128)(2,1)S(1)}, bf16[1,27,64,2]{2,3,1,0:T(2,128)(2,1)}, u32[]{:S(2)}) copy-start(bf16[1,27,64,2]{2,3,1,0:T(2,128)(2,1)} %param.13) | copy-start | bytes 20740
  6.5 135.5 %all-reduce.13.cloned.1.call-start = ((), (), s32[]{:S(2)}) async-start(), calls=%async_computation | async-start | bytes 1048576 | tf_op jit(solution)/shard_map/psum | solution.py:160
  81.4 78.6 %copy-start.30 = (bf16[1,27,2,64]{3,2,1,0:T(2,128)(2,1)S(1)}, bf16[1,27,2,64]{3,2,1,0:T(2,128)(2,1)}, u32[]{:S(2)}) copy-start(bf16[1,27,2,64]{3,2,1,0:T(2,128)(2,1)} %param.11) | copy-start | bytes 20740
  82.9 280.1 %all-reduce.15.cloned.1.call-start = ((), (), s32[]{:S(2)}) async-start(), calls=%async_computation.1 | async-start | bytes 1048576 | tf_op jit(solution)/shard_map/psum | solution.py:160
  142.9 6.5 collective-permute-start
  146.9 4.9 collective-permute-start.1
  152.1 7.9 %collective-permute-start.2 = (bf16[4,1,18,2,128]{4,3,2,1,0:T(2,128)(2,1)S(1)}, bf16[4,1,18,2,128]{4,3,2,1,0:T(2,128)(2,1)S(1)}, u32[]{:S(2)}, u32[]{:S(2)}) collective-permute-start(bf16[4,1,18,2,128]{4,3,2,1,0:T(2,128)(2,1)S(1)} %get-tuple-element.61), channel_id=1, source_target_pairs={{0,1},{1,2},{2,3},{3,4},{4,5},{5,6},{6,7},{8,9},{9,10},{10,11},{11... | collective-permute-start | bytes 110600 | tf_op jit(solution)/shard_map/ppermute | solution.py:12
  156.7 6.2 collective-permute-start.3
  170.6 5.9 collective-permute-start.4
  174.5 6.3 collective-permute-start.5
  183.3 54.9 %collective-permute-start.6 = (bf16[4,1,18,64,128]{4,3,2,1,0:T(8,128)(2,1)}, bf16[4,1,18,64,128]{4,3,2,1,0:T(8,128)(2,1)}, u32[]{:S(2)}, u32[]{:S(2)}) collective-permute-start(bf16[4,1,18,64,128]{4,3,2,1,0:T(8,128)(2,1)} %get-tuple-element.19), channel_id=1, source_target_pairs={{0,1},{1,2},{2,3},{3,4},{4,5},{5,6},{6,7},{8,9},{9,10},{10,11},{11... | collective-permute-start | bytes 3538952 | tf_op jit(solution)/shard_map/ppermute | solution.py:12
  187.3 53.9 %collective-permute-start.7 = (bf16[4,1,18,64,128]{4,3,2,1,0:T(8,128)(2,1)S(1)}, bf16[4,1,18,64,128]{4,3,2,1,0:T(8,128)(2,1)}, u32[]{:S(2)}, u32[]{:S(2)}) collective-permute-start(bf16[4,1,18,64,128]{4,3,2,1,0:T(8,128)(2,1)S(1)} %get-tuple-element.20), channel_id=1, source_target_pairs={{1,0},{2,1},{3,2},{4,3},{5,4},{6,5},{7,6},{9,8},{10,9},{11,10},{12... | collective-permute-start | bytes 3538952 | tf_op jit(solution)/shard_map/ppermute | solution.py:15
  271.6 13.6 %collective-permute-start.8 = (bf16[4,2,128,2,128]{4,3,2,1,0:T(2,128)(2,1)}, bf16[4,2,128,2,128]{4,3,2,1,0:T(2,128)(2,1)}, u32[]{:S(2)}, u32[]{:S(2)}) collective-permute-start(bf16[4,2,128,2,128]{4,3,2,1,0:T(2,128)(2,1)} %all_gather.6), channel_id=1, source_target_pairs={{0,64},{1,65},{2,66},{3,67},{4,68},{5,69},{6,70},{7,71},{8,72},{9,... | collective-permute-start | bytes 1572872 | tf_op jit(solution)/shard_map/ppermute | solution.py:23
  302.9 280.4 %all-reduce.17.cloned.1.call-start = ((), (), s32[]{:S(2)}) async-start(), calls=%async_computation.2 | async-start | bytes 1048576 | tf_op jit(solution)/shard_map/psum | solution.py:160
  363.9 6.5 collective-permute-start.10
  368.4 3.1 collective-permute-start.9
  371.7 8.1 %collective-permute-start.11 = (bf16[4,1,18,2,128]{4,3,2,1,0:T(2,128)(2,1)S(1)}, bf16[4,1,18,2,128]{4,3,2,1,0:T(2,128)(2,1)S(1)}, u32[]{:S(2)}, u32[]{:S(2)}) collective-permute-start(bf16[4,1,18,2,128]{4,3,2,1,0:T(2,128)(2,1)S(1)} %get-tuple-element.57), channel_id=1, source_target_pairs={{0,1},{1,2},{2,3},{3,4},{4,5},{5,6},{6,7},{8,9},{9,10},{10,11},{11... | collective-permute-start | bytes 110600 | tf_op jit(solution)/shard_map/ppermute | solution.py:12
  376.3 6.3 collective-permute-start.12
  390.8 8.2 %collective-permute-start.13 = (bf16[4,2,1,64,128]{4,3,2,1,0:T(8,128)(2,1)S(1)}, bf16[4,2,1,64,128]{4,3,2,1,0:T(8,128)(2,1)S(1)}, u32[]{:S(2)}, u32[]{:S(2)}) collective-permute-start(bf16[4,2,1,64,128]{4,3,2,1,0:T(8,128)(2,1)S(1)} %get-tuple-element.26), channel_id=1, source_target_pairs={{0,8},{8,16},{16,24},{24,32},{32,40},{40,48},{48,56},{1,9},{9,17},... | collective-permute-start | bytes 393224 | tf_op jit(solution)/shard_map/ppermute | solution.py:12
  395.9 6.3 collective-permute-start.14
  404.4 53.8 %collective-permute-start.15 = (bf16[4,1,18,64,128]{4,3,2,1,0:T(8,128)(2,1)}, bf16[4,1,18,64,128]{4,3,2,1,0:T(8,128)(2,1)}, u32[]{:S(2)}, u32[]{:S(2)}) collective-permute-start(bf16[4,1,18,64,128]{4,3,2,1,0:T(8,128)(2,1)} %get-tuple-element.17), channel_id=1, source_target_pairs={{0,1},{1,2},{2,3},{3,4},{4,5},{5,6},{6,7},{8,9},{9,10},{10,11},{11... | collective-permute-start | bytes 3538952 | tf_op jit(solution)/shard_map/ppermute | solution.py:12
  408.3 53.8 %collective-permute-start.16 = (bf16[4,1,18,64,128]{4,3,2,1,0:T(8,128)(2,1)}, bf16[4,1,18,64,128]{4,3,2,1,0:T(8,128)(2,1)}, u32[]{:S(2)}, u32[]{:S(2)}) collective-permute-start(bf16[4,1,18,64,128]{4,3,2,1,0:T(8,128)(2,1)} %get-tuple-element.18), channel_id=1, source_target_pairs={{1,0},{2,1},{3,2},{4,3},{5,4},{6,5},{7,6},{9,8},{10,9},{11,10},{12... | collective-permute-start | bytes 3538952 | tf_op jit(solution)/shard_map/ppermute | solution.py:15
  475.5 20.6 %copy-start.4 = (bf16[1,2,4,2,128,2,128]{6,5,4,3,2,1,0:T(2,128)(2,1)S(1)}, bf16[1,2,4,2,128,2,128]{6,5,4,3,2,1,0:T(2,128)(2,1)}, u32[]{:S(2)}) copy-start(bf16[1,2,4,2,128,2,128]{6,5,4,3,2,1,0:T(2,128)(2,1)} %get-tuple-element.23) | copy-start | bytes 3145732
  493.0 13.6 %collective-permute-start.17 = (bf16[4,2,128,2,128]{4,3,2,1,0:T(2,128)(2,1)}, bf16[4,2,128,2,128]{4,3,2,1,0:T(2,128)(2,1)}, u32[]{:S(2)}, u32[]{:S(2)}) collective-permute-start(bf16[4,2,128,2,128]{4,3,2,1,0:T(2,128)(2,1)} %all_gather.7), channel_id=1, source_target_pairs={{0,64},{1,65},{2,66},{3,67},{4,68},{5,69},{6,70},{7,71},{8,72},{9,... | collective-permute-start | bytes 1572872 | tf_op jit(solution)/shard_map/ppermute | solution.py:23
  584.2 6.5 collective-permute-start.18
  588.2 4.9 collective-permute-start.19
  593.3 7.9 %collective-permute-start.20 = (bf16[4,1,18,2,128]{4,3,2,1,0:T(2,128)(2,1)S(1)}, bf16[4,1,18,2,128]{4,3,2,1,0:T(2,128)(2,1)S(1)}, u32[]{:S(2)}, u32[]{:S(2)}) collective-permute-start(bf16[4,1,18,2,128]{4,3,2,1,0:T(2,128)(2,1)S(1)} %get-tuple-element.53), channel_id=1, source_target_pairs={{0,1},{1,2},{2,3},{3,4},{4,5},{5,6},{6,7},{8,9},{9,10},{10,11},{11... | collective-permute-start | bytes 110600 | tf_op jit(solution)/shard_map/ppermute | solution.py:12
  598.0 6.2 collective-permute-start.21
  612.3 5.9 collective-permute-start.22
  616.2 6.3 collective-permute-start.23
  624.3 54.9 %collective-permute-start.24 = (bf16[4,1,18,64,128]{4,3,2,1,0:T(8,128)(2,1)}, bf16[4,1,18,64,128]{4,3,2,1,0:T(8,128)(2,1)}, u32[]{:S(2)}, u32[]{:S(2)}) collective-permute-start(bf16[4,1,18,64,128]{4,3,2,1,0:T(8,128)(2,1)} %get-tuple-element.15), channel_id=1, source_target_pairs={{0,1},{1,2},{2,3},{3,4},{4,5},{5,6},{6,7},{8,9},{9,10},{10,11},{11... | collective-permute-start | bytes 3538952 | tf_op jit(solution)/shard_map/ppermute | solution.py:12
  628.3 53.9 %collective-permute-start.25 = (bf16[4,1,18,64,128]{4,3,2,1,0:T(8,128)(2,1)S(1)}, bf16[4,1,18,64,128]{4,3,2,1,0:T(8,128)(2,1)}, u32[]{:S(2)}, u32[]{:S(2)}) collective-permute-start(bf16[4,1,18,64,128]{4,3,2,1,0:T(8,128)(2,1)S(1)} %get-tuple-element.16), channel_id=1, source_target_pairs={{1,0},{2,1},{3,2},{4,3},{5,4},{6,5},{7,6},{9,8},{10,9},{11,10},{12... | collective-permute-start | bytes 3538952 | tf_op jit(solution)/shard_map/ppermute | solution.py:15
  (28 other events, 147.6 us)
Sparse Core Ops, SparseCore 0:
  83.0 58.9 all-reduce.12
  303.0 59.8 all-reduce.14
  524.2 59.0 all-reduce.16
where the time goes:
time: 713 us; the launch traced here: 706 us
  waiting for transfers between devices  369 us (52%)
  local copies, waits for them, and re-layouts  132 us (19%)
  starting transfers between devices  92.6 us (13%)
  matrix products  37.7 us (5%)
  other arithmetic  32.4 us (5%)
  blocking collectives  26.6 us (4%)
  between operations  14.9 us (2%)
    psum x3, waiting for transfers between devices, cascade(): summed = lax.psum(terms.astype(jnp.bfloat16), 'coil').astype(jnp.float32)  178 us
    ppermute x12, waiting for transfers between devices, extended(): lax.ppermute(lax.slice_in_dim(block, block.shape[dim] - width, None, axis...  142 us
    ppermute x12, starting transfers between devices, extended(): lax.ppermute(lax.slice_in_dim(block, block.shape[dim] - width, None, axis...  48.5 us
    ppermute x12, starting transfers between devices, extended(): lax.ppermute(lax.slice_in_dim(block, 0, width, axis=dim), axis, backward)  37.7 us
    ppermute x12, waiting for transfers between devices, extended(): lax.ppermute(lax.slice_in_dim(block, 0, width, axis=dim), axis, backward)  35.2 us
    convert_element_type x2, local copies, waits for them, and re-layouts, row_matrix(): return blocks.reshape(2 * length, 2 * length).astype(jnp.bfloat16)  26.9 us
    all_gather x2, blocking collectives, per_device(): assembled = lax.all_gather(output, 'coil', axis=2, tiled=True)  26.6 us
    dot_general x2, local copies, waits for them, and re-layouts, project(): jnp.einsum('prlie,tio->prltoe', edged, weights, preferred_element_type=jn...  19.1 us
  transfers between devices with their start and end apart: 29, of which 20 were waited for; matrix products, arithmetic and copies ran while one was open for 1% of the time, Pallas kernels for 0%

commit v1 on v0

--- a/solution.py
+++ b/solution.py
@@ -157,7 +157,7 @@
     back_half = along_rows(mixed, inverse_rows).astype(jnp.bfloat16)
     restored = along_columns(back_half, inverse_columns)
     terms = jnp.sum(multiply(coil_maps[:, None], restored, True), axis=0)
-    summed = lax.psum(terms.astype(jnp.bfloat16), "coil").astype(jnp.float32)
+    summed = jnp.sum(lax.all_gather(terms.astype(jnp.bfloat16), "coil"), axis=0).astype(jnp.float32)
     line_share = summed.shape[2] // lax.axis_size("coil")
     combined = lax.dynamic_slice_in_dim(summed, lax.axis_index("coil") * line_share, line_share, 2)
     combined = combined.astype(jnp.bfloat16)

time: 713 us -> 629 us (0.88)
  waiting for transfers between devices: 369 us -> 296 us
  local copies, waits for them, and re-layouts: 132 us -> 122 us
    psum x3 -> x0, waiting for transfers between devices: 178 us -> none  [cascade(): summed = lax.psum(terms.astype(jnp.bfloat16), 'coil').astype(jnp.float32)]
    all_gather x0 -> x3, waiting for transfers between devices: none -> 102 us  [cascade(): lax.all_gather(terms.astype(jnp.bfloat16), 'coil')]
    transpose x1 -> x0, local copies, waits for them, and re-layouts: 9.56 us -> none  [project(): jnp.einsum('prlie,tio->prltoe', edged, weights, preferred_element_type=jn...]
    reduce_sum x0 -> x3, other arithmetic: none -> 8.86 us  [cascade(): jnp.sum(lax.all_gather(terms.astype(jnp.bfloat16), 'coil'), axis=0)]
    dot_general x2 -> x3, local copies, waits for them, and re-layouts: 19.1 us -> 25.4 us  [project(): jnp.einsum('prlie,tio->prltoe', edged, weights, preferred_element_type=jn...]
where the time goes in v1:
time: 629 us; the launch traced here: 621 us
  waiting for transfers between devices  296 us (47%)
  local copies, waits for them, and re-layouts  122 us (19%)
  starting transfers between devices  86.5 us (14%)
  matrix products  44.3 us (7%)
  other arithmetic  31.8 us (5%)
  blocking collectives  26.5 us (4%)
  between operations  14.8 us (2%)
    ppermute x12, waiting for transfers between devices, extended(): lax.ppermute(lax.slice_in_dim(block, block.shape[dim] - width, None, axis...  142 us
    all_gather x3, waiting for transfers between devices, cascade(): lax.all_gather(terms.astype(jnp.bfloat16), 'coil')  102 us
    ppermute x12, starting transfers between devices, extended(): lax.ppermute(lax.slice_in_dim(block, block.shape[dim] - width, None, axis...  46.3 us
    ppermute x12, waiting for transfers between devices, extended(): lax.ppermute(lax.slice_in_dim(block, 0, width, axis=dim), axis, backward)  37.1 us
    ppermute x12, starting transfers between devices, extended(): lax.ppermute(lax.slice_in_dim(block, 0, width, axis=dim), axis, backward)  33.8 us
    convert_element_type x2, local copies, waits for them, and re-layouts, row_matrix(): return blocks.reshape(2 * length, 2 * length).astype(jnp.bfloat16)  26.9 us
    all_gather x2, blocking collectives, per_device(): assembled = lax.all_gather(output, 'coil', axis=2, tiled=True)  26.5 us
    dot_general x3, local copies, waits for them, and re-layouts, project(): jnp.einsum('prlie,tio->prltoe', edged, weights, preferred_element_type=jn...  25.4 us
  transfers between devices with their start and end apart: 29, of which 20 were waited for; matrix products, arithmetic and copies ran while one was open for 1% of the time, Pallas kernels for 0%

profile of v1, /device:TPU:35, one launch (start us, length us, event | category | flops | bytes accessed | tf_op | source)
XLA Modules:
  0.0 621.3 jit_solution(18316035264572097617)
XLA Ops:
  27.8 6.1 copy.228
  33.9 13.1 %reshape.491 = bf16[256,256,1]{1,0,2:T(8,128)(2,1)S(1)} reshape(bf16[128,2,128,2]{3,2,1,0:T(8,128)(2,1)} %copy.228) | data formatting | bytes 262144 | tf_op jit(solution)/shard_map/convert_element_type | solution.py:39
  47.0 6.1 copy.232
  53.1 13.8 %reshape.492 = bf16[256,256,1]{1,0,2:T(8,128)(2,1)} reshape(bf16[128,2,128,2]{3,2,1,0:T(8,128)(2,1)} %copy.232) | data formatting | bytes 262144 | tf_op jit(solution)/shard_map/convert_element_type | solution.py:39
  84.4 33.6 %all-gather.7.cloned.1.call-done = bf16[32,2,128,2,128]{4,2,3,1,0:T(8,128)(2,1)} async-done(((bf16[4,2,128,2,128]{4,2,3,1,0:T(8,128)(2,1)}), bf16[32,2,128,2,128]{4,2,3,1,0:T(8,128)(2,1)}) %all-gather.7.cloned.1.call-update) | async-done | bytes 4194320 | tf_op jit(solution)/shard_map/all_gather | solution.py:160
  129.1 4.6 collective-permute-start.2
  151.1 4.3 collective-permute-done.5
  157.9 3.9 collective-permute-start.6
  165.8 47.4 %collective-permute-done.6 = bf16[4,1,18,64,128]{4,3,2,1,0:T(8,128)(2,1)} collective-permute-done((bf16[4,1,18,64,128]{4,3,2,1,0:T(8,128)(2,1)}, bf16[4,1,18,64,128]{4,3,2,1,0:T(8,128)(2,1)}, u32[]{:S(2)}, u32[]{:S(2)}) %collective-permute-start.6) | collective-permute-done | bytes 1179680 | tf_op jit(solution)/shard_map/ppermute | solution.py:12
  215.6 6.0 fusion
  221.7 8.5 %copy.325 = f32[4,4,18,128,27,2]{3,2,5,1,0,4:T(8,128)S(1)} copy(f32[4,4,18,128,27,2]{3,4,5,2,1,0:T(8,128)} %fusion) | data formatting | bytes 15925248 | tf_op jit(solution)/shard_map/prlie,tio->prltoe/dot_general | solution.py:129
  231.8 13.2 %all_gather.19 = bf16[4,2,128,2,128]{4,2,3,1,0:T(8,128)(2,1)} all-gather(bf16[4,2,16,2,128]{4,2,3,1,0:T(8,128)(2,1)S(1)} %get-tuple-element.8), channel_id=1, replica_groups=mesh['cascade'=2,'coil'=8,'readout'=8] {'coil'}, dimensions={2}, use_global_device_ids=true | all-gather | bytes 589824 | tf_op jit(solution)/shard_map/all_gather | solution.py:204
  253.3 5.4 collective-permute-done.8
  274.7 34.4 %all-gather.9.cloned.1.call-done = bf16[32,2,128,2,128]{4,2,3,1,0:T(8,128)(2,1)} async-done(((bf16[4,2,128,2,128]{4,2,3,1,0:T(8,128)(2,1)}), bf16[32,2,128,2,128]{4,2,3,1,0:T(8,128)(2,1)}) %all-gather.9.cloned.1.call-update) | async-done | bytes 4194320 | tf_op jit(solution)/shard_map/all_gather | solution.py:160
  318.6 4.6 collective-permute-start.11
  335.6 5.6 collective-permute-start.13
  343.1 4.3 collective-permute-done.14
  349.7 3.9 collective-permute-start.15
  353.6 4.2 collective-permute-start.16
  357.8 46.8 %collective-permute-done.15 = bf16[4,1,18,64,128]{4,3,2,1,0:T(8,128)(2,1)} collective-permute-done((bf16[4,1,18,64,128]{4,3,2,1,0:T(8,128)(2,1)}, bf16[4,1,18,64,128]{4,3,2,1,0:T(8,128)(2,1)}, u32[]{:S(2)}, u32[]{:S(2)}) %collective-permute-start.15) | collective-permute-done | bytes 1179680 | tf_op jit(solution)/shard_map/ppermute | solution.py:12
  407.5 6.0 fusion.9
  413.5 8.5 %copy.324 = f32[4,4,18,128,27,2]{3,2,5,1,0,4:T(8,128)S(1)} copy(f32[4,4,18,128,27,2]{3,4,5,2,1,0:T(8,128)} %fusion.9) | data formatting | bytes 15925248 | tf_op jit(solution)/shard_map/prlie,tio->prltoe/dot_general | solution.py:129
  424.3 13.3 %all_gather.21 = bf16[4,2,128,2,128]{4,2,3,1,0:T(8,128)(2,1)} all-gather(bf16[4,2,16,2,128]{4,2,3,1,0:T(8,128)(2,1)S(1)} %get-tuple-element.6), channel_id=1, replica_groups=mesh['cascade'=2,'coil'=8,'readout'=8] {'coil'}, dimensions={2}, use_global_device_ids=true | all-gather | bytes 589824 | tf_op jit(solution)/shard_map/all_gather | solution.py:204
  442.4 8.8 %collective-permute-done.17 = bf16[4,2,128,2,128]{4,2,3,1,0:T(8,128)(2,1)} collective-permute-done((bf16[4,2,128,2,128]{4,2,3,1,0:T(8,128)(2,1)}, bf16[4,2,128,2,128]{4,2,3,1,0:T(8,128)(2,1)}, u32[]{:S(2)}, u32[]{:S(2)}) %collective-permute-start.17) | collective-permute-done | bytes 524320 | tf_op jit(solution)/shard_map/ppermute | solution.py:23
  466.9 33.7 %all-gather.11.cloned.1.call-done = bf16[32,2,128,2,128]{4,2,3,1,0:T(8,128)(2,1)} async-done(((bf16[4,2,128,2,128]{4,2,3,1,0:T(8,128)(2,1)}), bf16[32,2,128,2,128]{4,2,3,1,0:T(8,128)(2,1)}) %all-gather.11.cloned.1.call-update) | async-done | bytes 4194320 | tf_op jit(solution)/shard_map/all_gather | solution.py:160
  511.7 4.6 collective-permute-start.20
  519.5 3.9 collective-permute-done.21
  534.3 4.1 collective-permute-done.23
  540.2 3.9 collective-permute-start.24
  547.9 47.5 %collective-permute-done.24 = bf16[4,1,18,64,128]{4,3,2,1,0:T(8,128)(2,1)} collective-permute-done((bf16[4,1,18,64,128]{4,3,2,1,0:T(8,128)(2,1)}, bf16[4,1,18,64,128]{4,3,2,1,0:T(8,128)(2,1)}, u32[]{:S(2)}, u32[]{:S(2)}) %collective-permute-start.24) | collective-permute-done | bytes 1179680 | tf_op jit(solution)/shard_map/ppermute | solution.py:12
  598.0 5.7 fusion.18
  603.7 8.5 %copy.323 = f32[4,4,18,128,27,2]{3,2,5,1,0,4:T(8,128)S(1)} copy(f32[4,4,18,128,27,2]{3,4,5,2,1,0:T(8,128)} %fusion.18) | data formatting | bytes 15925248 | tf_op jit(solution)/shard_map/prlie,tio->prltoe/dot_general | solution.py:129
  (315 shorter events, 187.8 us)
Async XLA Ops:
  6.5 209.1 %copy-start = (bf16[1,27,64,2]{2,3,1,0:T(2,128)(2,1)S(1)}, bf16[1,27,64,2]{2,3,1,0:T(2,128)(2,1)}, u32[]{:S(2)}) copy-start(bf16[1,27,64,2]{2,3,1,0:T(2,128)(2,1)} %param.13) | copy-start | bytes 20740
  6.5 111.4 %all-gather.7.cloned.1.call-start = ((), (), s32[]{:S(2)}) async-start(), calls=%async_computation | async-start | bytes 4718592 | tf_op jit(solution)/shard_map/all_gather | solution.py:160
  84.3 224.8 %all-gather.9.cloned.1.call-start = ((), (), s32[]{:S(2)}) async-start(), calls=%async_computation.1 | async-start | bytes 4718592 | tf_op jit(solution)/shard_map/all_gather | solution.py:160
  120.9 21.1 %copy-start.23 = (bf16[4,2,128,2,128]{4,2,3,1,0:T(8,128)(2,1)}, bf16[4,2,128,2,128]{4,2,3,1,0:T(8,128)(2,1)S(1)}, u32[]{:S(2)}) copy-start(bf16[4,2,128,2,128]{4,2,3,1,0:T(8,128)(2,1)S(1)} %reduce_sum.64) | copy-start | bytes 1572868
  121.0 5.0 collective-permute-start
  124.1 5.0 collective-permute-start.1
  129.1 8.3 %collective-permute-start.2 = (bf16[4,1,18,2,128]{4,2,3,1,0:T(8,128)(2,1)S(1)}, bf16[4,1,18,2,128]{4,2,3,1,0:T(8,128)(2,1)S(1)}, u32[]{:S(2)}, u32[]{:S(2)}) collective-permute-start(bf16[4,1,18,2,128]{4,2,3,1,0:T(8,128)(2,1)S(1)} %get-tuple-element.58), channel_id=1, source_target_pairs={{0,1},{1,2},{2,3},{3,4},{4,5},{5,6},{6,7},{8,9},{9,10},{10,11},{11... | collective-permute-start | bytes 110600 | tf_op jit(solution)/shard_map/ppermute | solution.py:12
  133.7 7.0 %collective-permute-start.3 = (bf16[4,1,18,2,128]{4,2,3,1,0:T(8,128)(2,1)S(1)}, bf16[4,1,18,2,128]{4,2,3,1,0:T(8,128)(2,1)S(1)}, u32[]{:S(2)}, u32[]{:S(2)}) collective-permute-start(bf16[4,1,18,2,128]{4,2,3,1,0:T(8,128)(2,1)S(1)} %get-tuple-element.59), channel_id=1, source_target_pairs={{1,0},{2,1},{3,2},{4,3},{5,4},{6,5},{7,6},{9,8},{10,9},{11,10},{12... | collective-permute-start | bytes 110600 | tf_op jit(solution)/shard_map/ppermute | solution.py:15
  146.4 4.7 collective-permute-start.4
  149.1 6.3 %collective-permute-start.5 = (bf16[4,2,1,64,128]{4,3,2,1,0:T(8,128)(2,1)S(1)}, bf16[4,2,1,64,128]{4,3,2,1,0:T(8,128)(2,1)S(1)}, u32[]{:S(2)}, u32[]{:S(2)}) collective-permute-start(bf16[4,2,1,64,128]{4,3,2,1,0:T(8,128)(2,1)S(1)} %get-tuple-element.29), channel_id=1, source_target_pairs={{8,0},{16,8},{24,16},{32,24},{40,32},{48,40},{56,48},{9,1},{17,9},... | collective-permute-start | bytes 393224 | tf_op jit(solution)/shard_map/ppermute | solution.py:15
  157.9 55.2 %collective-permute-start.6 = (bf16[4,1,18,64,128]{4,3,2,1,0:T(8,128)(2,1)}, bf16[4,1,18,64,128]{4,3,2,1,0:T(8,128)(2,1)}, u32[]{:S(2)}, u32[]{:S(2)}) collective-permute-start(bf16[4,1,18,64,128]{4,3,2,1,0:T(8,128)(2,1)} %get-tuple-element.19), channel_id=1, source_target_pairs={{0,1},{1,2},{2,3},{3,4},{4,5},{5,6},{6,7},{8,9},{9,10},{10,11},{11... | collective-permute-start | bytes 3538952 | tf_op jit(solution)/shard_map/ppermute | solution.py:12
  161.8 53.8 %collective-permute-start.7 = (bf16[4,1,18,64,128]{4,3,2,1,0:T(8,128)(2,1)S(1)}, bf16[4,1,18,64,128]{4,3,2,1,0:T(8,128)(2,1)}, u32[]{:S(2)}, u32[]{:S(2)}) collective-permute-start(bf16[4,1,18,64,128]{4,3,2,1,0:T(8,128)(2,1)S(1)} %get-tuple-element.20), channel_id=1, source_target_pairs={{1,0},{2,1},{3,2},{4,3},{5,4},{6,5},{7,6},{9,8},{10,9},{11,10},{12... | collective-permute-start | bytes 3538952 | tf_op jit(solution)/shard_map/ppermute | solution.py:15
  245.1 13.6 %collective-permute-start.8 = (bf16[4,2,128,2,128]{4,2,3,1,0:T(8,128)(2,1)}, bf16[4,2,128,2,128]{4,2,3,1,0:T(8,128)(2,1)}, u32[]{:S(2)}, u32[]{:S(2)}) collective-permute-start(bf16[4,2,128,2,128]{4,2,3,1,0:T(8,128)(2,1)} %all_gather.19), channel_id=1, source_target_pairs={{0,64},{1,65},{2,66},{3,67},{4,68},{5,69},{6,70},{7,71},{8,72},{9,... | collective-permute-start | bytes 1572872 | tf_op jit(solution)/shard_map/ppermute | solution.py:23
  274.6 226.0 %all-gather.11.cloned.1.call-start = ((), (), s32[]{:S(2)}) async-start(), calls=%async_computation.2 | async-start | bytes 4718592 | tf_op jit(solution)/shard_map/all_gather | solution.py:160
  312.1 5.6 collective-permute-start.10
  314.3 4.2 collective-permute-start.9
  318.6 8.0 %collective-permute-start.11 = (bf16[4,1,18,2,128]{4,2,3,1,0:T(8,128)(2,1)S(1)}, bf16[4,1,18,2,128]{4,2,3,1,0:T(8,128)(2,1)S(1)}, u32[]{:S(2)}, u32[]{:S(2)}) collective-permute-start(bf16[4,1,18,2,128]{4,2,3,1,0:T(8,128)(2,1)S(1)} %get-tuple-element.56), channel_id=1, source_target_pairs={{0,1},{1,2},{2,3},{3,4},{4,5},{5,6},{6,7},{8,9},{9,10},{10,11},{11... | collective-permute-start | bytes 110600 | tf_op jit(solution)/shard_map/ppermute | solution.py:12
  323.2 6.3 %collective-permute-start.12 = (bf16[4,1,18,2,128]{4,2,3,1,0:T(8,128)(2,1)S(1)}, bf16[4,1,18,2,128]{4,2,3,1,0:T(8,128)(2,1)S(1)}, u32[]{:S(2)}, u32[]{:S(2)}) collective-permute-start(bf16[4,1,18,2,128]{4,2,3,1,0:T(8,128)(2,1)S(1)} %get-tuple-element.57), channel_id=1, source_target_pairs={{1,0},{2,1},{3,2},{4,3},{5,4},{6,5},{7,6},{9,8},{10,9},{11,10},{12... | collective-permute-start | bytes 110600 | tf_op jit(solution)/shard_map/ppermute | solution.py:15
  335.6 7.6 %collective-permute-start.13 = (bf16[4,2,1,64,128]{4,3,2,1,0:T(8,128)(2,1)S(1)}, bf16[4,2,1,64,128]{4,3,2,1,0:T(8,128)(2,1)S(1)}, u32[]{:S(2)}, u32[]{:S(2)}) collective-permute-start(bf16[4,2,1,64,128]{4,3,2,1,0:T(8,128)(2,1)S(1)} %get-tuple-element.26), channel_id=1, source_target_pairs={{0,8},{8,16},{16,24},{24,32},{32,40},{40,48},{48,56},{1,9},{9,17},... | collective-permute-start | bytes 393224 | tf_op jit(solution)/shard_map/ppermute | solution.py:12
  341.2 6.3 %collective-permute-start.14 = (bf16[4,2,1,64,128]{4,3,2,1,0:T(8,128)(2,1)S(1)}, bf16[4,2,1,64,128]{4,3,2,1,0:T(8,128)(2,1)S(1)}, u32[]{:S(2)}, u32[]{:S(2)}) collective-permute-start(bf16[4,2,1,64,128]{4,3,2,1,0:T(8,128)(2,1)S(1)} %get-tuple-element.27), channel_id=1, source_target_pairs={{8,0},{16,8},{24,16},{32,24},{40,32},{48,40},{56,48},{9,1},{17,9},... | collective-permute-start | bytes 393224 | tf_op jit(solution)/shard_map/ppermute | solution.py:15
  349.7 54.9 %collective-permute-start.15 = (bf16[4,1,18,64,128]{4,3,2,1,0:T(8,128)(2,1)}, bf16[4,1,18,64,128]{4,3,2,1,0:T(8,128)(2,1)}, u32[]{:S(2)}, u32[]{:S(2)}) collective-permute-start(bf16[4,1,18,64,128]{4,3,2,1,0:T(8,128)(2,1)} %get-tuple-element.17), channel_id=1, source_target_pairs={{0,1},{1,2},{2,3},{3,4},{4,5},{5,6},{6,7},{8,9},{9,10},{10,11},{11... | collective-permute-start | bytes 3538952 | tf_op jit(solution)/shard_map/ppermute | solution.py:12
  353.6 53.9 %collective-permute-start.16 = (bf16[4,1,18,64,128]{4,3,2,1,0:T(8,128)(2,1)}, bf16[4,1,18,64,128]{4,3,2,1,0:T(8,128)(2,1)}, u32[]{:S(2)}, u32[]{:S(2)}) collective-permute-start(bf16[4,1,18,64,128]{4,3,2,1,0:T(8,128)(2,1)} %get-tuple-element.18), channel_id=1, source_target_pairs={{1,0},{2,1},{3,2},{4,3},{5,4},{6,5},{7,6},{9,8},{10,9},{11,10},{12... | collective-permute-start | bytes 3538952 | tf_op jit(solution)/shard_map/ppermute | solution.py:15
  437.6 13.6 %collective-permute-start.17 = (bf16[4,2,128,2,128]{4,2,3,1,0:T(8,128)(2,1)}, bf16[4,2,128,2,128]{4,2,3,1,0:T(8,128)(2,1)}, u32[]{:S(2)}, u32[]{:S(2)}) collective-permute-start(bf16[4,2,128,2,128]{4,2,3,1,0:T(8,128)(2,1)} %all_gather.21), channel_id=1, source_target_pairs={{0,64},{1,65},{2,66},{3,67},{4,68},{5,69},{6,70},{7,71},{8,72},{9,... | collective-permute-start | bytes 1572872 | tf_op jit(solution)/shard_map/ppermute | solution.py:23
  503.6 21.1 %copy-start.22 = (bf16[4,2,128,2,128]{4,2,3,1,0:T(8,128)(2,1)}, bf16[4,2,128,2,128]{4,2,3,1,0:T(8,128)(2,1)S(1)}, u32[]{:S(2)}) copy-start(bf16[4,2,128,2,128]{4,2,3,1,0:T(8,128)(2,1)S(1)} %reduce_sum.68) | copy-start | bytes 1572868
  503.6 5.0 collective-permute-start.18
  506.7 5.0 collective-permute-start.19
  511.7 7.7 %collective-permute-start.20 = (bf16[4,1,18,2,128]{4,2,3,1,0:T(8,128)(2,1)S(1)}, bf16[4,1,18,2,128]{4,2,3,1,0:T(8,128)(2,1)S(1)}, u32[]{:S(2)}, u32[]{:S(2)}) collective-permute-start(bf16[4,1,18,2,128]{4,2,3,1,0:T(8,128)(2,1)S(1)} %get-tuple-element.54), channel_id=1, source_target_pairs={{0,1},{1,2},{2,3},{3,4},{4,5},{5,6},{6,7},{8,9},{9,10},{10,11},{11... | collective-permute-start | bytes 110600 | tf_op jit(solution)/shard_map/ppermute | solution.py:12
  516.4 7.0 %collective-permute-start.21 = (bf16[4,1,18,2,128]{4,2,3,1,0:T(8,128)(2,1)S(1)}, bf16[4,1,18,2,128]{4,2,3,1,0:T(8,128)(2,1)S(1)}, u32[]{:S(2)}, u32[]{:S(2)}) collective-permute-start(bf16[4,1,18,2,128]{4,2,3,1,0:T(8,128)(2,1)S(1)} %get-tuple-element.55), channel_id=1, source_target_pairs={{1,0},{2,1},{3,2},{4,3},{5,4},{6,5},{7,6},{9,8},{10,9},{11,10},{12... | collective-permute-start | bytes 110600 | tf_op jit(solution)/shard_map/ppermute | solution.py:15
  529.4 4.9 collective-permute-start.22
  532.1 6.3 %collective-permute-start.23 = (bf16[4,2,1,64,128]{4,3,2,1,0:T(8,128)(2,1)S(1)}, bf16[4,2,1,64,128]{4,3,2,1,0:T(8,128)(2,1)S(1)}, u32[]{:S(2)}, u32[]{:S(2)}) collective-permute-start(bf16[4,2,1,64,128]{4,3,2,1,0:T(8,128)(2,1)S(1)} %get-tuple-element.22), channel_id=1, source_target_pairs={{8,0},{16,8},{24,16},{32,24},{40,32},{48,40},{56,48},{9,1},{17,9},... | collective-permute-start | bytes 393224 | tf_op jit(solution)/shard_map/ppermute | solution.py:15
  540.2 55.2 %collective-permute-start.24 = (bf16[4,1,18,64,128]{4,3,2,1,0:T(8,128)(2,1)}, bf16[4,1,18,64,128]{4,3,2,1,0:T(8,128)(2,1)}, u32[]{:S(2)}, u32[]{:S(2)}) collective-permute-start(bf16[4,1,18,64,128]{4,3,2,1,0:T(8,128)(2,1)} %get-tuple-element.15), channel_id=1, source_target_pairs={{0,1},{1,2},{2,3},{3,4},{4,5},{5,6},{6,7},{8,9},{9,10},{10,11},{11... | collective-permute-start | bytes 3538952 | tf_op jit(solution)/shard_map/ppermute | solution.py:12
  544.2 53.8 %collective-permute-start.25 = (bf16[4,1,18,64,128]{4,3,2,1,0:T(8,128)(2,1)S(1)}, bf16[4,1,18,64,128]{4,3,2,1,0:T(8,128)(2,1)}, u32[]{:S(2)}, u32[]{:S(2)}) collective-permute-start(bf16[4,1,18,64,128]{4,3,2,1,0:T(8,128)(2,1)S(1)} %get-tuple-element.16), channel_id=1, source_target_pairs={{1,0},{2,1},{3,2},{4,3},{5,4},{6,5},{7,6},{9,8},{10,9},{11,10},{12... | collective-permute-start | bytes 3538952 | tf_op jit(solution)/shard_map/ppermute | solution.py:15
  (32 other events, 191.3 us)
Sparse Core Ops, SparseCore 0:
  84.4 33.4 all-gather.6
  274.8 34.3 all-gather.8
  467.1 33.5 all-gather.10
